TPU v7x, 32 devices: a whole 2x2x4 slice. The times are simulated.
32 devices in a mesh: section: 4 (over y, x), rep: 8 (over z, core).
Axes of the slice: x: 2, y: 2, z: 4, core: 2. Of those that a mesh axis runs over, the one named last changes fastest.
Arguments:
- inputs: bfloat16 [6, 256, 6144], P(None, 'rep'), may hold values from -6 to 6
- cotangent: bfloat16 [6, 256, 6144], P(None, 'rep'), may hold values from -6 to 6
- in_weight: bfloat16 [4, 6144, 256], P('section', 'rep'), may hold values from -0.078125 to 0.078125
- out_weight: bfloat16 [4, 6144, 256], P('section', 'rep'), may hold values from -0.375 to 0.375
- norm_gain: float32 [4, 6144], P('section'), may hold values from 0.5 to 1.5
- lengths: int32 [8, 6], P('rep'), may hold values from 1 to 32, 144 in all within a row
Outputs:
- grad_in_weight: bfloat16 [4, 6144, 256], P('section', 'rep')
- grad_out_weight: bfloat16 [4, 6144, 256], P('section', 'rep')
- grad_gain: float32 [4, 6144], P('section')
- grad_inputs: bfloat16 [4, 6, 256, 6144], P('section', None, 'rep')
Inputs may be any that keep to these rules, and one draw needn't show every extreme that they name: `lengths`: each replica's 6 counts sum to 144 and the largest is 32.
All inputs are finite; a program needn't handle non-finite values.
Results may differ from a plain program's by a relative error of at most 0.025.
Values may be sent and summed in bfloat16 or wider, within the bound.
A program may use at most 64 MiB of HBM per device.

v0:
```python
import math
import jax
import jax.numpy as jnp
from jax import lax
from jax.sharding import PartitionSpec as P

norm_epsilon = 1e-05


def from_behind(block, axis, distance):
    devices = range(lax.axis_size(axis))
    route = [(i - distance, i) for i in devices if i - distance in devices]
    return lax.ppermute(block, axis, route)


def section_forward(hidden, norm_gain, in_weight, out_weight):
    widened = hidden.astype(jnp.float32)
    inverse = lax.rsqrt(jnp.mean(widened * widened, axis=-1, keepdims=True) + norm_epsilon)
    normed = (widened * inverse * norm_gain).astype(jnp.bfloat16)
    before = jnp.dot(normed, in_weight, preferred_element_type=jnp.float32)
    activated = jax.nn.silu(before).astype(jnp.bfloat16)
    mixed = lax.dot_general(
        activated, out_weight, (((1,), (1,)), ((), ())), preferred_element_type=jnp.float32
    )
    return ((widened + mixed).astype(jnp.bfloat16), normed, before, activated)


def section_backward(hidden, norm_gain, in_weight, out_weight, before, upstream):
    widened = hidden.astype(jnp.float32)
    inverse = lax.rsqrt(jnp.mean(widened * widened, axis=-1, keepdims=True) + norm_epsilon)
    grad_activated = jnp.dot(upstream, out_weight, preferred_element_type=jnp.float32)
    sigmoid_value = jax.nn.sigmoid(before)
    grad_before = (grad_activated * sigmoid_value * (1.0 + before * (1.0 - sigmoid_value))).astype(
        jnp.bfloat16
    )
    grad_normed = lax.dot_general(
        grad_before, in_weight, (((1,), (1,)), ((), ())), preferred_element_type=jnp.float32
    )
    grad_scaled = grad_normed * norm_gain
    projection = jnp.mean(grad_scaled * widened, axis=-1, keepdims=True)
    grad_hidden = (
        upstream.astype(jnp.float32)
        + inverse * grad_scaled
        - widened * (inverse * inverse * inverse) * projection
    )
    gain_terms = jnp.sum(grad_normed * widened * inverse, axis=0)
    return (grad_hidden.astype(jnp.bfloat16), grad_before, gain_terms)


def write_slot(holders, contents, slot):
    return tuple(
        (
            lax.dynamic_update_index_in_dim(holder, content, slot, 0)
            for holder, content in zip(holders, contents)
        )
    )


def body(inputs, cotangent, in_weight, out_weight, norm_gain, lengths):
    section_count = lax.axis_size("section")
    replicas = lax.axis_size("rep")
    position = lax.axis_index("section")
    micro_count, tok_rows, width = inputs.shape
    grad_scale = 1.0 / math.sqrt(micro_count * tok_rows * replicas)
    gain_row = norm_gain[0]
    full_in, full_out = (
        lax.all_gather(in_weight[0], "rep", axis=0, tiled=True),
        lax.all_gather(out_weight[0], "rep", axis=0, tiled=True),
    )
    rank_width = full_in.shape[1]
    tick_total = micro_count + section_count - 1
    blank = jnp.zeros((tok_rows, width), jnp.bfloat16)
    wide_zeros = jnp.zeros((micro_count, tok_rows, width), jnp.bfloat16)
    narrow_zeros = jnp.zeros((micro_count, tok_rows, rank_width), jnp.bfloat16)
    stores = (wide_zeros,)

    def forward_tick(moment, carried):
        received, holders = carried
        micro = moment - position
        active = (micro >= 0) & (micro < micro_count)
        slot = jnp.clip(micro, 0, micro_count - 1)
        fresh = lax.dynamic_index_in_dim(inputs, slot, 0, keepdims=False)
        entering = jnp.where(position == 0, fresh, received)

        def forward_run_section(holders):
            leaving, normed, before, activated = section_forward(
                entering, gain_row, full_in, full_out
            )
            contents = (entering,)
            return (leaving, write_slot(holders, contents, slot))

        def forward_skip_section(holders):
            return (blank, holders)

        leaving, holders = lax.cond(active, forward_run_section, forward_skip_section, holders)
        received = from_behind(leaving, "section", 1)
        return (received, holders)

    received, stores = lax.fori_loop(0, tick_total, forward_tick, (blank, stores))
    keep_rows = jnp.arange(tok_rows, dtype=jnp.int32)[None, :] < lengths[0][:, None]
    seeds = jnp.where(keep_rows[:, :, None], cotangent, jnp.zeros((), jnp.bfloat16))
    gain_start = jnp.zeros((width,), jnp.float32)
    buffers = (wide_zeros, narrow_zeros, wide_zeros, wide_zeros, narrow_zeros)

    def backward_tick(moment, carried):
        received, holders, gain_total = carried
        micro = moment - (section_count - 1 - position)
        active = (micro >= 0) & (micro < micro_count)
        slot = jnp.clip(micro, 0, micro_count - 1)
        seed_rows = lax.dynamic_index_in_dim(seeds, slot, 0, keepdims=False)
        entering = jnp.where(position == section_count - 1, seed_rows, received)

        def backward_run_section(operands):
            holders, gain_total = operands
            hidden_rows = lax.dynamic_index_in_dim(stores[0], slot, 0, keepdims=False)
            unused, normed, before, activated = section_forward(
                hidden_rows, gain_row, full_in, full_out
            )
            grad_hidden, grad_before, gain_terms = section_backward(
                hidden_rows, gain_row, full_in, full_out, before, entering
            )
            contents = (grad_hidden, grad_before, entering, normed, activated)
            return (grad_hidden, (write_slot(holders, contents, slot), gain_total + gain_terms))

        def backward_skip_section(operands):
            return (blank, operands)

        leaving, (holders, gain_total) = lax.cond(
            active, backward_run_section, backward_skip_section, (holders, gain_total)
        )
        received = from_behind(leaving, "section", -1)
        return (received, holders, gain_total)

    received, buffers, gain_total = lax.fori_loop(
        0, tick_total, backward_tick, (blank, buffers, gain_start)
    )
    normed_all = buffers[3]
    activated_all = buffers[4]
    flat_rows = micro_count * tok_rows
    normed_flat = normed_all.reshape(flat_rows, width)
    upstream_flat = buffers[2].reshape(flat_rows, width)
    before_flat = buffers[1].reshape(flat_rows, rank_width)
    activated_flat = activated_all.reshape(flat_rows, rank_width)
    left_term = lax.dot_general(
        normed_flat, before_flat, (((0,), (0,)), ((), ())), preferred_element_type=jnp.float32
    )
    right_term = lax.dot_general(
        upstream_flat, activated_flat, (((0,), (0,)), ((), ())), preferred_element_type=jnp.float32
    )
    summed = lax.psum_scatter(
        (jnp.concatenate((left_term, right_term), axis=1) * grad_scale).astype(jnp.bfloat16),
        "rep",
        scatter_dimension=0,
        tiled=True,
    ).astype(jnp.float32)
    grad_in_weight = summed[:, :rank_width].astype(jnp.bfloat16)[None]
    grad_out_weight = summed[:, rank_width:].astype(jnp.bfloat16)[None]
    grad_gain = lax.psum(gain_total * grad_scale, "rep")[None]
    grad_inputs = buffers[0][None]
    return (grad_in_weight, grad_out_weight, grad_gain, grad_inputs)


def solution(mesh):
    in_specs = (
        P(None, "rep", None),
        P(None, "rep", None),
        P("section", "rep", None),
        P("section", "rep", None),
        P("section", None),
        P("rep", None),
    )
    out_specs = (
        P("section", "rep", None),
        P("section", "rep", None),
        P("section", None),
        P("section", None, "rep", None),
    )
    return jax.shard_map(body, mesh=mesh, in_specs=in_specs, out_specs=out_specs, check_vma=False)
```

profile of v0, /device:TPU:0, one launch (start us, length us, event | category | flops | bytes accessed | tf_op | source)
XLA Modules:
  0.0 532.2 jit_solution(10388793744136409346)
XLA Ops:
  12.8 37.8 %all-gather.5.cloned.1.call-done = bf16[1,6144,256]{2,1,0:T(8,128)(2,1)} async-done(((bf16[1,768,256]{2,1,0:T(8,128)(2,1)}), bf16[1,6144,256]{2,1,0:T(8,128)(2,1)}) %all-gather.5.cloned.1.call-update) | async-done | bytes 3145744 | tf_op jit(solution)/shard_map/all_gather | solution.py:67
  50.6 38.8 %all-gather.7.cloned.1.call-done = bf16[1,6144,256]{2,1,0:T(8,128)(2,1)} async-done(((bf16[1,768,256]{2,1,0:T(8,128)(2,1)}), bf16[1,6144,256]{2,1,0:T(8,128)(2,1)}) %all-gather.7.cloned.1.call-update) | async-done | bytes 3145744 | tf_op jit(solution)/shard_map/all_gather | solution.py:68
  89.7 159.5 %while.46 = (s32[]{:T(128)}, bf16[32,6144]{1,0:T(8,128)(2,1)S(1)}, bf16[6,32,6144]{2,1,0:T(8,128)(2,1)S(1)}, s32[]{:T(128)}, pred[]{:T(512)}, /*index=5*/bf16[6,...) while((s32[]{:T(128)}, bf16[32,6144]{1,0:T(8,128)(2,1)S(1)}, ...), condition=%wide.region_4.5_spmd, body=%wide.region_0.4_spmd.sunk | while | flops 203530272 | bytes 12215116 | solution.py:99
  89.7 6.5 %conditional.4 = (bf16[32,6144]{1,0:T(8,128)(2,1)S(1)}, bf16[6,32,6144]{2,1,0:T(8,128)(2,1)S(1)}) conditional(s32[]{:T(128)} %convert_element_type.183, bf16[6,32,6144]{2,1,0:T(8,128)(2,1)S(1)} %get-tuple-element.1063, (pred[]{:T(512)}, s32[]{:T(128)}, bf16[6,32,6144]{2,1,0:T(8,128)(2,1)}, bf16[32,6144]{1,0:T(8,128)(2,1)S(1)}, ...), branch_computations={%region_1.1_spmd, %region_2.3_spmd} | conditional | flops 203530272 | bytes 9069101 | solution.py:95
  91.1 5.2 fusion
  98.3 9.3 %collective-permute-done = bf16[32,6144]{1,0:T(8,128)(2,1)S(1)} collective-permute-done((bf16[32,6144]{1,0:T(8,128)(2,1)}, bf16[32,6144]{1,0:T(8,128)(2,1)S(1)}, u32[]{:S(2)}, u32[]{:S(2)}) %collective-permute-start) | collective-permute-done | bytes 393248 | tf_op jit(solution)/shard_map/while/body/eval_jaxpr/ppermute | solution.py:13
  107.6 6.5 %conditional.4 = (bf16[32,6144]{1,0:T(8,128)(2,1)S(1)}, bf16[6,32,6144]{2,1,0:T(8,128)(2,1)S(1)}) conditional(s32[]{:T(128)} %convert_element_type.183, bf16[6,32,6144]{2,1,0:T(8,128)(2,1)S(1)} %get-tuple-element.1063, (pred[]{:T(512)}, s32[]{:T(128)}, bf16[6,32,6144]{2,1,0:T(8,128)(2,1)}, bf16[32,6144]{1,0:T(8,128)(2,1)S(1)}, ...), branch_computations={%region_1.1_spmd, %region_2.3_spmd} | conditional | flops 203530272 | bytes 9069101 | solution.py:95
  108.9 5.1 fusion
  114.8 4.3 collective-permute-start
  119.2 8.5 %collective-permute-done = bf16[32,6144]{1,0:T(8,128)(2,1)S(1)} collective-permute-done((bf16[32,6144]{1,0:T(8,128)(2,1)}, bf16[32,6144]{1,0:T(8,128)(2,1)S(1)}, u32[]{:S(2)}, u32[]{:S(2)}) %collective-permute-start) | collective-permute-done | bytes 393248 | tf_op jit(solution)/shard_map/while/body/eval_jaxpr/ppermute | solution.py:13
  127.6 6.5 %conditional.4 = (bf16[32,6144]{1,0:T(8,128)(2,1)S(1)}, bf16[6,32,6144]{2,1,0:T(8,128)(2,1)S(1)}) conditional(s32[]{:T(128)} %convert_element_type.183, bf16[6,32,6144]{2,1,0:T(8,128)(2,1)S(1)} %get-tuple-element.1063, (pred[]{:T(512)}, s32[]{:T(128)}, bf16[6,32,6144]{2,1,0:T(8,128)(2,1)}, bf16[32,6144]{1,0:T(8,128)(2,1)S(1)}, ...), branch_computations={%region_1.1_spmd, %region_2.3_spmd} | conditional | flops 203530272 | bytes 9069101 | solution.py:95
  128.9 5.2 fusion
  139.2 7.6 %collective-permute-done = bf16[32,6144]{1,0:T(8,128)(2,1)S(1)} collective-permute-done((bf16[32,6144]{1,0:T(8,128)(2,1)}, bf16[32,6144]{1,0:T(8,128)(2,1)S(1)}, u32[]{:S(2)}, u32[]{:S(2)}) %collective-permute-start) | collective-permute-done | bytes 393248 | tf_op jit(solution)/shard_map/while/body/eval_jaxpr/ppermute | solution.py:13
  146.8 6.5 %conditional.4 = (bf16[32,6144]{1,0:T(8,128)(2,1)S(1)}, bf16[6,32,6144]{2,1,0:T(8,128)(2,1)S(1)}) conditional(s32[]{:T(128)} %convert_element_type.183, bf16[6,32,6144]{2,1,0:T(8,128)(2,1)S(1)} %get-tuple-element.1063, (pred[]{:T(512)}, s32[]{:T(128)}, bf16[6,32,6144]{2,1,0:T(8,128)(2,1)}, bf16[32,6144]{1,0:T(8,128)(2,1)S(1)}, ...), branch_computations={%region_1.1_spmd, %region_2.3_spmd} | conditional | flops 203530272 | bytes 9069101 | solution.py:95
  148.1 5.2 fusion
  158.3 6.8 %collective-permute-done = bf16[32,6144]{1,0:T(8,128)(2,1)S(1)} collective-permute-done((bf16[32,6144]{1,0:T(8,128)(2,1)}, bf16[32,6144]{1,0:T(8,128)(2,1)S(1)}, u32[]{:S(2)}, u32[]{:S(2)}) %collective-permute-start) | collective-permute-done | bytes 393248 | tf_op jit(solution)/shard_map/while/body/eval_jaxpr/ppermute | solution.py:13
  165.1 6.5 %conditional.4 = (bf16[32,6144]{1,0:T(8,128)(2,1)S(1)}, bf16[6,32,6144]{2,1,0:T(8,128)(2,1)S(1)}) conditional(s32[]{:T(128)} %convert_element_type.183, bf16[6,32,6144]{2,1,0:T(8,128)(2,1)S(1)} %get-tuple-element.1063, (pred[]{:T(512)}, s32[]{:T(128)}, bf16[6,32,6144]{2,1,0:T(8,128)(2,1)}, bf16[32,6144]{1,0:T(8,128)(2,1)S(1)}, ...), branch_computations={%region_1.1_spmd, %region_2.3_spmd} | conditional | flops 203530272 | bytes 9069101 | solution.py:95
  166.4 5.2 fusion
  172.3 4.5 collective-permute-start
  176.9 6.2 %collective-permute-done = bf16[32,6144]{1,0:T(8,128)(2,1)S(1)} collective-permute-done((bf16[32,6144]{1,0:T(8,128)(2,1)}, bf16[32,6144]{1,0:T(8,128)(2,1)S(1)}, u32[]{:S(2)}, u32[]{:S(2)}) %collective-permute-start) | collective-permute-done | bytes 393248 | tf_op jit(solution)/shard_map/while/body/eval_jaxpr/ppermute | solution.py:13
  183.0 6.5 %conditional.4 = (bf16[32,6144]{1,0:T(8,128)(2,1)S(1)}, bf16[6,32,6144]{2,1,0:T(8,128)(2,1)S(1)}) conditional(s32[]{:T(128)} %convert_element_type.183, bf16[6,32,6144]{2,1,0:T(8,128)(2,1)S(1)} %get-tuple-element.1063, (pred[]{:T(512)}, s32[]{:T(128)}, bf16[6,32,6144]{2,1,0:T(8,128)(2,1)}, bf16[32,6144]{1,0:T(8,128)(2,1)S(1)}, ...), branch_computations={%region_1.1_spmd, %region_2.3_spmd} | conditional | flops 203530272 | bytes 9069101 | solution.py:95
  184.3 5.2 fusion
  190.3 5.2 collective-permute-start
  195.5 5.6 %collective-permute-done = bf16[32,6144]{1,0:T(8,128)(2,1)S(1)} collective-permute-done((bf16[32,6144]{1,0:T(8,128)(2,1)}, bf16[32,6144]{1,0:T(8,128)(2,1)S(1)}, u32[]{:S(2)}, u32[]{:S(2)}) %collective-permute-start) | collective-permute-done | bytes 393248 | tf_op jit(solution)/shard_map/while/body/eval_jaxpr/ppermute | solution.py:13
  201.8 11.7 %collective-permute-start = (bf16[32,6144]{1,0:T(8,128)(2,1)}, bf16[32,6144]{1,0:T(8,128)(2,1)S(1)}, u32[]{:S(2)}, u32[]{:S(2)}) collective-permute-start(bf16[32,6144]{1,0:T(8,128)(2,1)} %copy-done.5), channel_id=1, source_target_pairs={{0,8},{8,16},{16,24},{1,9},{9,17},{17,25},{2,10},{10,18},{18,26},{... | collective-permute-start | bytes 1179656 | tf_op jit(solution)/shard_map/while/body/eval_jaxpr/ppermute | solution.py:13
  213.5 5.6 %collective-permute-done = bf16[32,6144]{1,0:T(8,128)(2,1)S(1)} collective-permute-done((bf16[32,6144]{1,0:T(8,128)(2,1)}, bf16[32,6144]{1,0:T(8,128)(2,1)S(1)}, u32[]{:S(2)}, u32[]{:S(2)}) %collective-permute-start) | collective-permute-done | bytes 393248 | tf_op jit(solution)/shard_map/while/body/eval_jaxpr/ppermute | solution.py:13
  219.8 5.2 collective-permute-start
  225.0 5.6 %collective-permute-done = bf16[32,6144]{1,0:T(8,128)(2,1)S(1)} collective-permute-done((bf16[32,6144]{1,0:T(8,128)(2,1)}, bf16[32,6144]{1,0:T(8,128)(2,1)S(1)}, u32[]{:S(2)}, u32[]{:S(2)}) %collective-permute-start) | collective-permute-done | bytes 393248 | tf_op jit(solution)/shard_map/while/body/eval_jaxpr/ppermute | solution.py:13
  231.4 12.2 %collective-permute-start = (bf16[32,6144]{1,0:T(8,128)(2,1)}, bf16[32,6144]{1,0:T(8,128)(2,1)S(1)}, u32[]{:S(2)}, u32[]{:S(2)}) collective-permute-start(bf16[32,6144]{1,0:T(8,128)(2,1)} %copy-done.5), channel_id=1, source_target_pairs={{0,8},{8,16},{16,24},{1,9},{9,17},{17,25},{2,10},{10,18},{18,26},{... | collective-permute-start | bytes 1179656 | tf_op jit(solution)/shard_map/while/body/eval_jaxpr/ppermute | solution.py:13
  243.6 5.6 %collective-permute-done = bf16[32,6144]{1,0:T(8,128)(2,1)S(1)} collective-permute-done((bf16[32,6144]{1,0:T(8,128)(2,1)}, bf16[32,6144]{1,0:T(8,128)(2,1)S(1)}, u32[]{:S(2)}, u32[]{:S(2)}) %collective-permute-start) | collective-permute-done | bytes 393248 | tf_op jit(solution)/shard_map/while/body/eval_jaxpr/ppermute | solution.py:13
  255.9 191.4 %while.47 = (s32[]{:T(128)}, bf16[32,6144]{1,0:T(8,128)(2,1)}, bf16[6,32,6144]{2,1,0:T(8,128)(2,1)}, bf16[6,32,256]{2,1,0:T(8,128)(2,1)S(1)}, bf16[6,32,6144]{2,...) while((s32[]{:T(128)}, bf16[32,6144]{1,0:T(8,128)(2,1)}, ...), condition=%wide.region_11.12_spmd, body=%wide.region_5.11_spmd.sunk | while | flops 307413088 | bytes 30610964 | solution.py:134
  257.9 9.9 %collective-permute-done.1 = bf16[32,6144]{1,0:T(8,128)(2,1)} collective-permute-done((bf16[32,6144]{1,0:T(8,128)(2,1)}, bf16[32,6144]{1,0:T(8,128)(2,1)}, u32[]{:S(2)}, u32[]{:S(2)}) %collective-permute-start.1) | collective-permute-done | bytes 393248 | tf_op jit(solution)/shard_map/while/body/eval_jaxpr/ppermute | solution.py:13
  269.9 11.7 %collective-permute-done.1 = bf16[32,6144]{1,0:T(8,128)(2,1)} collective-permute-done((bf16[32,6144]{1,0:T(8,128)(2,1)}, bf16[32,6144]{1,0:T(8,128)(2,1)}, u32[]{:S(2)}, u32[]{:S(2)}) %collective-permute-start.1) | collective-permute-done | bytes 393248 | tf_op jit(solution)/shard_map/while/body/eval_jaxpr/ppermute | solution.py:13
  283.7 36.6 %collective-permute-done.1 = bf16[32,6144]{1,0:T(8,128)(2,1)} collective-permute-done((bf16[32,6144]{1,0:T(8,128)(2,1)}, bf16[32,6144]{1,0:T(8,128)(2,1)}, u32[]{:S(2)}, u32[]{:S(2)}) %collective-permute-start.1) | collective-permute-done | bytes 393248 | tf_op jit(solution)/shard_map/while/body/eval_jaxpr/ppermute | solution.py:13
  320.3 10.2 %conditional.5 = (bf16[32,6144]{1,0:T(8,128)(2,1)}, bf16[6,32,6144]{2,1,0:T(8,128)(2,1)}, bf16[6,32,256]{2,1,0:T(8,128)(2,1)S(1)}, bf16[6,32,6144]{2,1,0:T(8,128...) conditional(s32[]{:T(128)} %convert_element_type.184, ...), branch_computations={%region_6.6_spmd, %region_7.10_spmd} | conditional | flops 307413088 | bytes 29037696 | solution.py:128
  331.8 9.6 %collective-permute-done.1 = bf16[32,6144]{1,0:T(8,128)(2,1)} collective-permute-done((bf16[32,6144]{1,0:T(8,128)(2,1)}, bf16[32,6144]{1,0:T(8,128)(2,1)}, u32[]{:S(2)}, u32[]{:S(2)}) %collective-permute-start.1) | collective-permute-done | bytes 393248 | tf_op jit(solution)/shard_map/while/body/eval_jaxpr/ppermute | solution.py:13
  341.4 10.2 %conditional.5 = (bf16[32,6144]{1,0:T(8,128)(2,1)}, bf16[6,32,6144]{2,1,0:T(8,128)(2,1)}, bf16[6,32,256]{2,1,0:T(8,128)(2,1)S(1)}, bf16[6,32,6144]{2,1,0:T(8,128...) conditional(s32[]{:T(128)} %convert_element_type.184, ...), branch_computations={%region_6.6_spmd, %region_7.10_spmd} | conditional | flops 307413088 | bytes 29037696 | solution.py:128
  352.9 9.6 %collective-permute-done.1 = bf16[32,6144]{1,0:T(8,128)(2,1)} collective-permute-done((bf16[32,6144]{1,0:T(8,128)(2,1)}, bf16[32,6144]{1,0:T(8,128)(2,1)}, u32[]{:S(2)}, u32[]{:S(2)}) %collective-permute-start.1) | collective-permute-done | bytes 393248 | tf_op jit(solution)/shard_map/while/body/eval_jaxpr/ppermute | solution.py:13
  362.5 10.2 %conditional.5 = (bf16[32,6144]{1,0:T(8,128)(2,1)}, bf16[6,32,6144]{2,1,0:T(8,128)(2,1)}, bf16[6,32,256]{2,1,0:T(8,128)(2,1)S(1)}, bf16[6,32,6144]{2,1,0:T(8,128...) conditional(s32[]{:T(128)} %convert_element_type.184, ...), branch_computations={%region_6.6_spmd, %region_7.10_spmd} | conditional | flops 307413088 | bytes 29037696 | solution.py:128
  374.0 9.6 %collective-permute-done.1 = bf16[32,6144]{1,0:T(8,128)(2,1)} collective-permute-done((bf16[32,6144]{1,0:T(8,128)(2,1)}, bf16[32,6144]{1,0:T(8,128)(2,1)}, u32[]{:S(2)}, u32[]{:S(2)}) %collective-permute-start.1) | collective-permute-done | bytes 393248 | tf_op jit(solution)/shard_map/while/body/eval_jaxpr/ppermute | solution.py:13
  383.6 10.3 %conditional.5 = (bf16[32,6144]{1,0:T(8,128)(2,1)}, bf16[6,32,6144]{2,1,0:T(8,128)(2,1)}, bf16[6,32,256]{2,1,0:T(8,128)(2,1)S(1)}, bf16[6,32,6144]{2,1,0:T(8,128...) conditional(s32[]{:T(128)} %convert_element_type.184, ...), branch_computations={%region_6.6_spmd, %region_7.10_spmd} | conditional | flops 307413088 | bytes 29037696 | solution.py:128
  395.2 9.6 %collective-permute-done.1 = bf16[32,6144]{1,0:T(8,128)(2,1)} collective-permute-done((bf16[32,6144]{1,0:T(8,128)(2,1)}, bf16[32,6144]{1,0:T(8,128)(2,1)}, u32[]{:S(2)}, u32[]{:S(2)}) %collective-permute-start.1) | collective-permute-done | bytes 393248 | tf_op jit(solution)/shard_map/while/body/eval_jaxpr/ppermute | solution.py:13
  404.8 10.3 %conditional.5 = (bf16[32,6144]{1,0:T(8,128)(2,1)}, bf16[6,32,6144]{2,1,0:T(8,128)(2,1)}, bf16[6,32,256]{2,1,0:T(8,128)(2,1)S(1)}, bf16[6,32,6144]{2,1,0:T(8,128...) conditional(s32[]{:T(128)} %convert_element_type.184, ...), branch_computations={%region_6.6_spmd, %region_7.10_spmd} | conditional | flops 307413088 | bytes 29037696 | solution.py:128
  416.3 10.7 %collective-permute-done.1 = bf16[32,6144]{1,0:T(8,128)(2,1)} collective-permute-done((bf16[32,6144]{1,0:T(8,128)(2,1)}, bf16[32,6144]{1,0:T(8,128)(2,1)}, u32[]{:S(2)}, u32[]{:S(2)}) %collective-permute-start.1) | collective-permute-done | bytes 393248 | tf_op jit(solution)/shard_map/while/body/eval_jaxpr/ppermute | solution.py:13
  427.0 10.3 %conditional.5 = (bf16[32,6144]{1,0:T(8,128)(2,1)}, bf16[6,32,6144]{2,1,0:T(8,128)(2,1)}, bf16[6,32,256]{2,1,0:T(8,128)(2,1)S(1)}, bf16[6,32,6144]{2,1,0:T(8,128...) conditional(s32[]{:T(128)} %convert_element_type.184, ...), branch_computations={%region_6.6_spmd, %region_7.10_spmd} | conditional | flops 307413088 | bytes 29037696 | solution.py:128
  438.6 8.7 %collective-permute-done.1 = bf16[32,6144]{1,0:T(8,128)(2,1)} collective-permute-done((bf16[32,6144]{1,0:T(8,128)(2,1)}, bf16[32,6144]{1,0:T(8,128)(2,1)}, u32[]{:S(2)}, u32[]{:S(2)}) %collective-permute-start.1) | collective-permute-done | bytes 393248 | tf_op jit(solution)/shard_map/while/body/eval_jaxpr/ppermute | solution.py:13
  455.0 27.8 %psum.7 = f32[1,6144]{1,0:T(1,128)} all-reduce(f32[1,6144]{1,0:T(1,128)S(1)} %bitcast.83), channel_id=1, replica_groups=mesh['section'=4,'rep'=8] {'rep'}, use_global_device_ids=true, to_apply=%region_13.14 | all-reduce | flops 6144 | bytes 49152 | tf_op jit(solution)/shard_map/psum | solution.py:158
  482.9 39.8 %reduce-scatter.2.cloned.1.call-done = bf16[768,512]{0,1:T(8,128)(2,1)} async-done(((bf16[6144,512]{0,1:T(8,128)(2,1)}), bf16[768,512]{0,1:T(8,128)(2,1)}) %reduce-scatter.2.cloned.1.call-update) | async-done | bytes 786448 | tf_op jit(solution)/shard_map/reduce_scatter | solution.py:150
  (158 shorter events, 125.4 us)
Async XLA Ops:
  7.2 43.4 %all-gather.5.cloned.1.call-start = ((), (), s32[]{:S(2)}) async-start(), calls=%async_computation.2 | async-start | bytes 3538944 | tf_op jit(solution)/shard_map/all_gather | solution.py:67
  7.9 81.5 %all-gather.7.cloned.1.call-start = ((), (), s32[]{:S(2)}) async-start(), calls=%async_computation.3 | async-start | bytes 3538944 | tf_op jit(solution)/shard_map/all_gather | solution.py:68
  8.6 514.0 %reduce-scatter.2.cloned.1.call-start = ((), (), s32[]{:S(2)}) async-start(), calls=%async_computation.1 | async-start | bytes 7077888 | tf_op jit(solution)/shard_map/reduce_scatter | solution.py:150
  12.8 76.9 %copy-start.3 = (f32[1,6144]{1,0:T(1,128)S(1)}, f32[1,6144]{1,0:T(1,128)}, u32[]{:S(2)}) copy-start(f32[1,6144]{1,0:T(1,128)} %param.18) | copy-start | bytes 73732
  96.2 0.8 copy-start.5
  97.0 10.6 %collective-permute-start = (bf16[32,6144]{1,0:T(8,128)(2,1)}, bf16[32,6144]{1,0:T(8,128)(2,1)S(1)}, u32[]{:S(2)}, u32[]{:S(2)}) collective-permute-start(bf16[32,6144]{1,0:T(8,128)(2,1)} %copy-done.5), channel_id=1, source_target_pairs={{0,8},{8,16},{16,24},{1,9},{9,17},{17,25},{2,10},{10,18},{18,26},{... | collective-permute-start | bytes 1179656 | tf_op jit(solution)/shard_map/while/body/eval_jaxpr/ppermute | solution.py:13
  114.1 0.8 copy-start.5
  114.8 12.8 %collective-permute-start = (bf16[32,6144]{1,0:T(8,128)(2,1)}, bf16[32,6144]{1,0:T(8,128)(2,1)S(1)}, u32[]{:S(2)}, u32[]{:S(2)}) collective-permute-start(bf16[32,6144]{1,0:T(8,128)(2,1)} %copy-done.5), channel_id=1, source_target_pairs={{0,8},{8,16},{16,24},{1,9},{9,17},{17,25},{2,10},{10,18},{18,26},{... | collective-permute-start | bytes 1179656 | tf_op jit(solution)/shard_map/while/body/eval_jaxpr/ppermute | solution.py:13
  134.1 0.8 copy-start.5
  134.9 11.9 %collective-permute-start = (bf16[32,6144]{1,0:T(8,128)(2,1)}, bf16[32,6144]{1,0:T(8,128)(2,1)S(1)}, u32[]{:S(2)}, u32[]{:S(2)}) collective-permute-start(bf16[32,6144]{1,0:T(8,128)(2,1)} %copy-done.5), channel_id=1, source_target_pairs={{0,8},{8,16},{16,24},{1,9},{9,17},{17,25},{2,10},{10,18},{18,26},{... | collective-permute-start | bytes 1179656 | tf_op jit(solution)/shard_map/while/body/eval_jaxpr/ppermute | solution.py:13
  153.2 0.8 copy-start.5
  154.0 11.1 %collective-permute-start = (bf16[32,6144]{1,0:T(8,128)(2,1)}, bf16[32,6144]{1,0:T(8,128)(2,1)S(1)}, u32[]{:S(2)}, u32[]{:S(2)}) collective-permute-start(bf16[32,6144]{1,0:T(8,128)(2,1)} %copy-done.5), channel_id=1, source_target_pairs={{0,8},{8,16},{16,24},{1,9},{9,17},{17,25},{2,10},{10,18},{18,26},{... | collective-permute-start | bytes 1179656 | tf_op jit(solution)/shard_map/while/body/eval_jaxpr/ppermute | solution.py:13
  171.5 0.8 copy-start.5
  172.3 10.7 %collective-permute-start = (bf16[32,6144]{1,0:T(8,128)(2,1)}, bf16[32,6144]{1,0:T(8,128)(2,1)S(1)}, u32[]{:S(2)}, u32[]{:S(2)}) collective-permute-start(bf16[32,6144]{1,0:T(8,128)(2,1)} %copy-done.5), channel_id=1, source_target_pairs={{0,8},{8,16},{16,24},{1,9},{9,17},{17,25},{2,10},{10,18},{18,26},{... | collective-permute-start | bytes 1179656 | tf_op jit(solution)/shard_map/while/body/eval_jaxpr/ppermute | solution.py:13
  189.5 0.8 copy-start.5
  190.3 10.8 %collective-permute-start = (bf16[32,6144]{1,0:T(8,128)(2,1)}, bf16[32,6144]{1,0:T(8,128)(2,1)S(1)}, u32[]{:S(2)}, u32[]{:S(2)}) collective-permute-start(bf16[32,6144]{1,0:T(8,128)(2,1)} %copy-done.5), channel_id=1, source_target_pairs={{0,8},{8,16},{16,24},{1,9},{9,17},{17,25},{2,10},{10,18},{18,26},{... | collective-permute-start | bytes 1179656 | tf_op jit(solution)/shard_map/while/body/eval_jaxpr/ppermute | solution.py:13
  201.1 0.7 copy-start.5
  201.8 17.2 %collective-permute-start = (bf16[32,6144]{1,0:T(8,128)(2,1)}, bf16[32,6144]{1,0:T(8,128)(2,1)S(1)}, u32[]{:S(2)}, u32[]{:S(2)}) collective-permute-start(bf16[32,6144]{1,0:T(8,128)(2,1)} %copy-done.5), channel_id=1, source_target_pairs={{0,8},{8,16},{16,24},{1,9},{9,17},{17,25},{2,10},{10,18},{18,26},{... | collective-permute-start | bytes 1179656 | tf_op jit(solution)/shard_map/while/body/eval_jaxpr/ppermute | solution.py:13
  219.1 0.7 copy-start.5
  219.8 10.8 %collective-permute-start = (bf16[32,6144]{1,0:T(8,128)(2,1)}, bf16[32,6144]{1,0:T(8,128)(2,1)S(1)}, u32[]{:S(2)}, u32[]{:S(2)}) collective-permute-start(bf16[32,6144]{1,0:T(8,128)(2,1)} %copy-done.5), channel_id=1, source_target_pairs={{0,8},{8,16},{16,24},{1,9},{9,17},{17,25},{2,10},{10,18},{18,26},{... | collective-permute-start | bytes 1179656 | tf_op jit(solution)/shard_map/while/body/eval_jaxpr/ppermute | solution.py:13
  230.6 0.7 copy-start.5
  231.4 17.8 %collective-permute-start = (bf16[32,6144]{1,0:T(8,128)(2,1)}, bf16[32,6144]{1,0:T(8,128)(2,1)S(1)}, u32[]{:S(2)}, u32[]{:S(2)}) collective-permute-start(bf16[32,6144]{1,0:T(8,128)(2,1)} %copy-done.5), channel_id=1, source_target_pairs={{0,8},{8,16},{16,24},{1,9},{9,17},{17,25},{2,10},{10,18},{18,26},{... | collective-permute-start | bytes 1179656 | tf_op jit(solution)/shard_map/while/body/eval_jaxpr/ppermute | solution.py:13
  249.2 1.6 copy-start.2
  252.4 3.4 copy-start
  256.6 11.2 %collective-permute-start.1 = (bf16[32,6144]{1,0:T(8,128)(2,1)}, bf16[32,6144]{1,0:T(8,128)(2,1)}, u32[]{:S(2)}, u32[]{:S(2)}) collective-permute-start(bf16[32,6144]{1,0:T(8,128)(2,1)} %get-tuple-element.1024), channel_id=1, source_target_pairs={{8,0},{16,8},{24,16},{9,1},{17,9},{25,17},{10,2},{18,10},{26,18},{... | collective-permute-start | bytes 1179656 | tf_op jit(solution)/shard_map/while/body/eval_jaxpr/ppermute | solution.py:13
  268.6 13.0 %collective-permute-start.1 = (bf16[32,6144]{1,0:T(8,128)(2,1)}, bf16[32,6144]{1,0:T(8,128)(2,1)}, u32[]{:S(2)}, u32[]{:S(2)}) collective-permute-start(bf16[32,6144]{1,0:T(8,128)(2,1)} %get-tuple-element.1024), channel_id=1, source_target_pairs={{8,0},{16,8},{24,16},{9,1},{17,9},{25,17},{10,2},{18,10},{26,18},{... | collective-permute-start | bytes 1179656 | tf_op jit(solution)/shard_map/while/body/eval_jaxpr/ppermute | solution.py:13
  282.4 37.9 %collective-permute-start.1 = (bf16[32,6144]{1,0:T(8,128)(2,1)}, bf16[32,6144]{1,0:T(8,128)(2,1)}, u32[]{:S(2)}, u32[]{:S(2)}) collective-permute-start(bf16[32,6144]{1,0:T(8,128)(2,1)} %get-tuple-element.1024), channel_id=1, source_target_pairs={{8,0},{16,8},{24,16},{9,1},{17,9},{25,17},{10,2},{18,10},{26,18},{... | collective-permute-start | bytes 1179656 | tf_op jit(solution)/shard_map/while/body/eval_jaxpr/ppermute | solution.py:13
  321.5 3.9 copy-start.1
  330.5 10.9 %collective-permute-start.1 = (bf16[32,6144]{1,0:T(8,128)(2,1)}, bf16[32,6144]{1,0:T(8,128)(2,1)}, u32[]{:S(2)}, u32[]{:S(2)}) collective-permute-start(bf16[32,6144]{1,0:T(8,128)(2,1)} %get-tuple-element.1024), channel_id=1, source_target_pairs={{8,0},{16,8},{24,16},{9,1},{17,9},{25,17},{10,2},{18,10},{26,18},{... | collective-permute-start | bytes 1179656 | tf_op jit(solution)/shard_map/while/body/eval_jaxpr/ppermute | solution.py:13
  342.6 3.9 copy-start.1
  351.7 10.8 %collective-permute-start.1 = (bf16[32,6144]{1,0:T(8,128)(2,1)}, bf16[32,6144]{1,0:T(8,128)(2,1)}, u32[]{:S(2)}, u32[]{:S(2)}) collective-permute-start(bf16[32,6144]{1,0:T(8,128)(2,1)} %get-tuple-element.1024), channel_id=1, source_target_pairs={{8,0},{16,8},{24,16},{9,1},{17,9},{25,17},{10,2},{18,10},{26,18},{... | collective-permute-start | bytes 1179656 | tf_op jit(solution)/shard_map/while/body/eval_jaxpr/ppermute | solution.py:13
  363.7 3.9 copy-start.1
  372.7 10.9 %collective-permute-start.1 = (bf16[32,6144]{1,0:T(8,128)(2,1)}, bf16[32,6144]{1,0:T(8,128)(2,1)}, u32[]{:S(2)}, u32[]{:S(2)}) collective-permute-start(bf16[32,6144]{1,0:T(8,128)(2,1)} %get-tuple-element.1024), channel_id=1, source_target_pairs={{8,0},{16,8},{24,16},{9,1},{17,9},{25,17},{10,2},{18,10},{26,18},{... | collective-permute-start | bytes 1179656 | tf_op jit(solution)/shard_map/while/body/eval_jaxpr/ppermute | solution.py:13
  384.8 3.9 copy-start.1
  393.9 10.9 %collective-permute-start.1 = (bf16[32,6144]{1,0:T(8,128)(2,1)}, bf16[32,6144]{1,0:T(8,128)(2,1)}, u32[]{:S(2)}, u32[]{:S(2)}) collective-permute-start(bf16[32,6144]{1,0:T(8,128)(2,1)} %get-tuple-element.1024), channel_id=1, source_target_pairs={{8,0},{16,8},{24,16},{9,1},{17,9},{25,17},{10,2},{18,10},{26,18},{... | collective-permute-start | bytes 1179656 | tf_op jit(solution)/shard_map/while/body/eval_jaxpr/ppermute | solution.py:13
  406.0 3.9 copy-start.1
  415.1 12.0 %collective-permute-start.1 = (bf16[32,6144]{1,0:T(8,128)(2,1)}, bf16[32,6144]{1,0:T(8,128)(2,1)}, u32[]{:S(2)}, u32[]{:S(2)}) collective-permute-start(bf16[32,6144]{1,0:T(8,128)(2,1)} %get-tuple-element.1024), channel_id=1, source_target_pairs={{8,0},{16,8},{24,16},{9,1},{17,9},{25,17},{10,2},{18,10},{26,18},{... | collective-permute-start | bytes 1179656 | tf_op jit(solution)/shard_map/while/body/eval_jaxpr/ppermute | solution.py:13
  428.2 3.9 copy-start.1
  437.3 10.0 %collective-permute-start.1 = (bf16[32,6144]{1,0:T(8,128)(2,1)}, bf16[32,6144]{1,0:T(8,128)(2,1)}, u32[]{:S(2)}, u32[]{:S(2)}) collective-permute-start(bf16[32,6144]{1,0:T(8,128)(2,1)} %get-tuple-element.1024), channel_id=1, source_target_pairs={{8,0},{16,8},{24,16},{9,1},{17,9},{25,17},{10,2},{18,10},{26,18},{... | collective-permute-start | bytes 1179656 | tf_op jit(solution)/shard_map/while/body/eval_jaxpr/ppermute | solution.py:13
  447.3 2.8 copy-start.4
Sparse Core Ops, SparseCore 0:
  9.6 40.9 all-gather.4
  52.2 37.1 all-gather.6
  455.2 67.4 reduce-scatter.1
where the time goes:
time: 534 us; the launch traced here: 532 us
  waiting for transfers between devices  294 us (55%)
  starting transfers between devices  64.6 us (12%)
  matrix products  63 us (12%)
  other arithmetic  48.9 us (9%)
  blocking collectives  27.8 us (5%)
  local copies, waits for them, and re-layouts  19.1 us (4%)
  between operations  13.8 us (3%)
    ppermute x18, waiting for transfers between devices, from_behind(): return lax.ppermute(block, axis, route)  177 us
    ppermute x18, starting transfers between devices, from_behind(): return lax.ppermute(block, axis, route)  64.5 us
    reduce_scatter x1, waiting for transfers between devices, body(): lax.psum_scatter((jnp.concatenate((left_term, right_term), axis=1) * grad...  39.8 us
    all_gather x1, waiting for transfers between devices, body(): lax.all_gather(out_weight[0], 'rep', axis=0, tiled=True)  38.8 us
    all_gather x1, waiting for transfers between devices, body(): lax.all_gather(in_weight[0], 'rep', axis=0, tiled=True)  37.8 us
    dynamic_update_slice x18, other arithmetic, write_slot(): lax.dynamic_update_index_in_dim(holder, content, slot, 0)  32.5 us
    dot_general x6, matrix products, section_forward(): lax.dot_general(activated, out_weight, (((1,), (1,)), ((), ())), preferre...  30.9 us
    psum x1, blocking collectives, body(): grad_gain = lax.psum(gain_total * grad_scale, 'rep')[None]  27.8 us
  transfers between devices with their start and end apart: 21, of which 21 were waited for; matrix products, arithmetic and copies ran while one was open for 1% of the time, Pallas kernels for 0%

commit v1 on v0

--- a/solution.py
+++ b/solution.py
@@ -5,6 +5,28 @@
 from jax.sharding import PartitionSpec as P
 
 norm_epsilon = 1e-05
+
+
+def in_order(parts, dim):
+    parts = jnp.moveaxis(parts, 0, dim)
+    shape = parts.shape
+    return parts.reshape(*shape[:dim], shape[dim] * shape[dim + 1], *shape[dim + 2 :])
+
+
+def collect(x, axis, dim):
+    devices = lax.axis_size(axis)
+    pairs = [(i, (i + 1) % devices) for i in range(devices)]
+    back = [(b, a) for a, b in pairs]
+    lower, upper = ([], [])
+    for step in range(devices - 1):
+        if step % 2 == 0:
+            lower.append(lax.ppermute(lower[-1] if lower else x, axis, pairs))
+        else:
+            upper.append(lax.ppermute(upper[-1] if upper else x, axis, back))
+    parts = jnp.stack([*lower[::-1], x, *upper])
+    shift = lax.axis_index(axis) - len(lower)
+    parts = parts[(jnp.arange(devices) - shift) % devices]
+    return in_order(parts, dim)
 
 
 def from_behind(block, axis, distance):
@@ -65,7 +87,7 @@
     gain_row = norm_gain[0]
     full_in, full_out = (
         lax.all_gather(in_weight[0], "rep", axis=0, tiled=True),
-        lax.all_gather(out_weight[0], "rep", axis=0, tiled=True),
+        collect(out_weight[0], "rep", 0),
     )
     rank_width = full_in.shape[1]
     tick_total = micro_count + section_count - 1

time: 534 us -> 552 us (1.034)
  waiting for transfers between devices: 294 us -> 261 us
  local copies, waits for them, and re-layouts: 19.1 us -> 33.9 us
  blocking collectives: 27.8 us -> 41.5 us
  starting transfers between devices: 64.6 us -> 77.1 us
    ppermute x0 -> x7, waiting for transfers between devices: none -> 45.9 us  [the longest x4 43.9 us: collect(): lower.append(lax.ppermute(lower[-1] if lower else x, axis, pairs))]
    all_gather x1 -> x0, waiting for transfers between devices: 38.8 us -> none  [body(): lax.all_gather(out_weight[0], 'rep', axis=0, tiled=True)]
    all_gather x1, waiting for transfers between devices: 37.8 us -> 0.02 us  [body(): lax.all_gather(in_weight[0], 'rep', axis=0, tiled=True)]
    psum x1, blocking collectives: 27.8 us -> 41.5 us  [body(): grad_gain = lax.psum(gain_total * grad_scale, 'rep')[None]]
    ppermute x0 -> x7, starting transfers between devices: none -> 11.5 us  [the longest x3 10.9 us: collect(): upper.append(lax.ppermute(upper[-1] if upper else x, axis, back))]
    unnamed x10 -> x21, local copies, waits for them, and re-layouts: 2.49 us -> 8.02 us
  transfers between devices with their start and end apart: 21 -> 27, of which waited for: 21 -> 25; matrix products, arithmetic and copies ran while one was open for 1% -> 2% of each run, Pallas kernels for 0% -> 0%
where the time goes in v1:
time: 552 us; the launch traced here: 550 us
  waiting for transfers between devices  261 us (47%)
  starting transfers between devices  77.1 us (14%)
  matrix products  68.2 us (12%)
  other arithmetic  53.7 us (10%)
  blocking collectives  41.5 us (8%)
  local copies, waits for them, and re-layouts  33.9 us (6%)
  between operations  14.1 us (3%)
    ppermute x18, waiting for transfers between devices, from_behind(): return lax.ppermute(block, axis, route)  173 us
    ppermute x18, starting transfers between devices, from_behind(): return lax.ppermute(block, axis, route)  65.5 us
    ppermute x4, waiting for transfers between devices, collect(): lower.append(lax.ppermute(lower[-1] if lower else x, axis, pairs))  43.9 us
    psum x1, blocking collectives, body(): grad_gain = lax.psum(gain_total * grad_scale, 'rep')[None]  41.5 us
    reduce_scatter x1, waiting for transfers between devices, body(): lax.psum_scatter((jnp.concatenate((left_term, right_term), axis=1) * grad...  41.1 us
    dynamic_update_slice x18, other arithmetic, write_slot(): lax.dynamic_update_index_in_dim(holder, content, slot, 0)  36.3 us
    dot_general x6, matrix products, section_forward(): lax.dot_general(activated, out_weight, (((1,), (1,)), ((), ())), preferre...  29.8 us
    dot_general x6, matrix products, section_forward(): before = jnp.dot(normed, in_weight, preferred_element_type=jnp.float32)  14 us
  transfers between devices with their start and end apart: 27, of which 25 were waited for; matrix products, arithmetic and copies ran while one was open for 2% of the time, Pallas kernels for 0%

profile of v1, /device:TPU:0, one launch (start us, length us, event | category | flops | bytes accessed | tf_op | source)
XLA Modules:
  0.0 550.3 jit_solution(1636127652764327891)
XLA Ops:
  8.5 9.7 %collective-permute-done.2 = bf16[768,256]{1,0:T(8,128)(2,1)S(1)} collective-permute-done((bf16[768,256]{1,0:T(8,128)(2,1)}, bf16[768,256]{1,0:T(8,128)(2,1)S(1)}, u32[]{:S(2)}, u32[]{:S(2)}) %collective-permute-start.2) | collective-permute-done | bytes 393248 | tf_op jit(solution)/shard_map/ppermute | solution.py:23
  21.7 14.7 %collective-permute-done.3 = bf16[768,256]{1,0:T(8,128)(2,1)S(1)} collective-permute-done((bf16[768,256]{1,0:T(8,128)(2,1)S(1)}, bf16[768,256]{1,0:T(8,128)(2,1)S(1)}, u32[]{:S(2)}, u32[]{:S(2)}) %collective-permute-start.3) | collective-permute-done | bytes 393248 | tf_op jit(solution)/shard_map/ppermute | solution.py:23
  42.6 13.3 %collective-permute-done.4 = bf16[768,256]{1,0:T(8,128)(2,1)S(1)} collective-permute-done((bf16[768,256]{1,0:T(8,128)(2,1)S(1)}, bf16[768,256]{1,0:T(8,128)(2,1)S(1)}, u32[]{:S(2)}, u32[]{:S(2)}) %collective-permute-start.4) | collective-permute-done | bytes 393248 | tf_op jit(solution)/shard_map/ppermute | solution.py:23
  63.3 6.2 %collective-permute-done.5 = bf16[768,256]{1,0:T(8,128)(2,1)S(1)} collective-permute-done((bf16[768,256]{1,0:T(8,128)(2,1)S(1)}, bf16[768,256]{1,0:T(8,128)(2,1)S(1)}, u32[]{:S(2)}, u32[]{:S(2)}) %collective-permute-start.5) | collective-permute-done | bytes 393248 | tf_op jit(solution)/shard_map/ppermute | solution.py:23
  80.8 159.6 %while.46 = (s32[]{:T(128)}, bf16[32,6144]{1,0:T(8,128)(2,1)}, bf16[6,32,6144]{2,1,0:T(8,128)(2,1)}, s32[]{:T(128)}, pred[]{:T(512)}, /*index=5*/bf16[6,32,6144]...) while((s32[]{:T(128)}, bf16[32,6144]{1,0:T(8,128)(2,1)}, ...), condition=%wide.region_4.5_spmd, body=%wide.region_0.4_spmd.sunk | while | flops 203530272 | bytes 12215627 | solution.py:121
  80.8 7.0 %conditional.4 = (bf16[32,6144]{1,0:T(8,128)(2,1)}, bf16[6,32,6144]{2,1,0:T(8,128)(2,1)}) conditional(s32[]{:T(128)} %convert_element_type.183, bf16[6,32,6144]{2,1,0:T(8,128)(2,1)} %get-tuple-element.1063, (pred[]{:T(512)}, s32[]{:T(128)}, bf16[6,32,6144]{2,1,0:T(8,128)(2,1)}, bf16[32,6144]{1,0:T(8,128)(2,1)}, f32[1,6144]{1,0:T(1,128)}, ...), branch_computations={%region_1.1_spmd, %region_2.3_spmd} | conditional | flops 203530272 | bytes 9069612 | solution.py:117
  82.8 5.0 fusion
  89.1 7.6 %collective-permute-done = bf16[32,6144]{1,0:T(8,128)(2,1)S(1)} collective-permute-done((bf16[32,6144]{1,0:T(8,128)(2,1)}, bf16[32,6144]{1,0:T(8,128)(2,1)S(1)}, u32[]{:S(2)}, u32[]{:S(2)}) %collective-permute-start) | collective-permute-done | bytes 393248 | tf_op jit(solution)/shard_map/while/body/eval_jaxpr/ppermute | solution.py:35
  97.5 7.0 %conditional.4 = (bf16[32,6144]{1,0:T(8,128)(2,1)}, bf16[6,32,6144]{2,1,0:T(8,128)(2,1)}) conditional(s32[]{:T(128)} %convert_element_type.183, bf16[6,32,6144]{2,1,0:T(8,128)(2,1)} %get-tuple-element.1063, (pred[]{:T(512)}, s32[]{:T(128)}, bf16[6,32,6144]{2,1,0:T(8,128)(2,1)}, bf16[32,6144]{1,0:T(8,128)(2,1)}, f32[1,6144]{1,0:T(1,128)}, ...), branch_computations={%region_1.1_spmd, %region_2.3_spmd} | conditional | flops 203530272 | bytes 9069612 | solution.py:117
  99.5 5.0 fusion
  108.9 6.7 %collective-permute-done = bf16[32,6144]{1,0:T(8,128)(2,1)S(1)} collective-permute-done((bf16[32,6144]{1,0:T(8,128)(2,1)}, bf16[32,6144]{1,0:T(8,128)(2,1)S(1)}, u32[]{:S(2)}, u32[]{:S(2)}) %collective-permute-start) | collective-permute-done | bytes 393248 | tf_op jit(solution)/shard_map/while/body/eval_jaxpr/ppermute | solution.py:35
  116.4 7.0 %conditional.4 = (bf16[32,6144]{1,0:T(8,128)(2,1)}, bf16[6,32,6144]{2,1,0:T(8,128)(2,1)}) conditional(s32[]{:T(128)} %convert_element_type.183, bf16[6,32,6144]{2,1,0:T(8,128)(2,1)} %get-tuple-element.1063, (pred[]{:T(512)}, s32[]{:T(128)}, bf16[6,32,6144]{2,1,0:T(8,128)(2,1)}, bf16[32,6144]{1,0:T(8,128)(2,1)}, f32[1,6144]{1,0:T(1,128)}, ...), branch_computations={%region_1.1_spmd, %region_2.3_spmd} | conditional | flops 203530272 | bytes 9069612 | solution.py:117
  118.4 5.0 fusion
  127.8 5.9 %collective-permute-done = bf16[32,6144]{1,0:T(8,128)(2,1)S(1)} collective-permute-done((bf16[32,6144]{1,0:T(8,128)(2,1)}, bf16[32,6144]{1,0:T(8,128)(2,1)S(1)}, u32[]{:S(2)}, u32[]{:S(2)}) %collective-permute-start) | collective-permute-done | bytes 393248 | tf_op jit(solution)/shard_map/while/body/eval_jaxpr/ppermute | solution.py:35
  134.4 7.0 %conditional.4 = (bf16[32,6144]{1,0:T(8,128)(2,1)}, bf16[6,32,6144]{2,1,0:T(8,128)(2,1)}) conditional(s32[]{:T(128)} %convert_element_type.183, bf16[6,32,6144]{2,1,0:T(8,128)(2,1)} %get-tuple-element.1063, (pred[]{:T(512)}, s32[]{:T(128)}, bf16[6,32,6144]{2,1,0:T(8,128)(2,1)}, bf16[32,6144]{1,0:T(8,128)(2,1)}, f32[1,6144]{1,0:T(1,128)}, ...), branch_computations={%region_1.1_spmd, %region_2.3_spmd} | conditional | flops 203530272 | bytes 9069612 | solution.py:117
  136.5 5.0 fusion
  145.9 5.6 %collective-permute-done = bf16[32,6144]{1,0:T(8,128)(2,1)S(1)} collective-permute-done((bf16[32,6144]{1,0:T(8,128)(2,1)}, bf16[32,6144]{1,0:T(8,128)(2,1)S(1)}, u32[]{:S(2)}, u32[]{:S(2)}) %collective-permute-start) | collective-permute-done | bytes 393248 | tf_op jit(solution)/shard_map/while/body/eval_jaxpr/ppermute | solution.py:35
  152.2 7.0 %conditional.4 = (bf16[32,6144]{1,0:T(8,128)(2,1)}, bf16[6,32,6144]{2,1,0:T(8,128)(2,1)}) conditional(s32[]{:T(128)} %convert_element_type.183, bf16[6,32,6144]{2,1,0:T(8,128)(2,1)} %get-tuple-element.1063, (pred[]{:T(512)}, s32[]{:T(128)}, bf16[6,32,6144]{2,1,0:T(8,128)(2,1)}, bf16[32,6144]{1,0:T(8,128)(2,1)}, f32[1,6144]{1,0:T(1,128)}, ...), branch_computations={%region_1.1_spmd, %region_2.3_spmd} | conditional | flops 203530272 | bytes 9069612 | solution.py:117
  154.3 5.0 fusion
  163.7 5.6 %collective-permute-done = bf16[32,6144]{1,0:T(8,128)(2,1)S(1)} collective-permute-done((bf16[32,6144]{1,0:T(8,128)(2,1)}, bf16[32,6144]{1,0:T(8,128)(2,1)S(1)}, u32[]{:S(2)}, u32[]{:S(2)}) %collective-permute-start) | collective-permute-done | bytes 393248 | tf_op jit(solution)/shard_map/while/body/eval_jaxpr/ppermute | solution.py:35
  170.0 7.0 %conditional.4 = (bf16[32,6144]{1,0:T(8,128)(2,1)}, bf16[6,32,6144]{2,1,0:T(8,128)(2,1)}) conditional(s32[]{:T(128)} %convert_element_type.183, bf16[6,32,6144]{2,1,0:T(8,128)(2,1)} %get-tuple-element.1063, (pred[]{:T(512)}, s32[]{:T(128)}, bf16[6,32,6144]{2,1,0:T(8,128)(2,1)}, bf16[32,6144]{1,0:T(8,128)(2,1)}, f32[1,6144]{1,0:T(1,128)}, ...), branch_computations={%region_1.1_spmd, %region_2.3_spmd} | conditional | flops 203530272 | bytes 9069612 | solution.py:117
  172.0 5.0 fusion
  177.0 5.3 collective-permute-start
  182.3 5.6 %collective-permute-done = bf16[32,6144]{1,0:T(8,128)(2,1)S(1)} collective-permute-done((bf16[32,6144]{1,0:T(8,128)(2,1)}, bf16[32,6144]{1,0:T(8,128)(2,1)S(1)}, u32[]{:S(2)}, u32[]{:S(2)}) %collective-permute-start) | collective-permute-done | bytes 393248 | tf_op jit(solution)/shard_map/while/body/eval_jaxpr/ppermute | solution.py:35
  189.4 11.6 %collective-permute-start = (bf16[32,6144]{1,0:T(8,128)(2,1)}, bf16[32,6144]{1,0:T(8,128)(2,1)S(1)}, u32[]{:S(2)}, u32[]{:S(2)}) collective-permute-start(bf16[32,6144]{1,0:T(8,128)(2,1)} %get-tuple-element.1007), channel_id=1, source_target_pairs={{0,8},{8,16},{16,24},{1,9},{9,17},{17,25},{2,10},{10,18},{18,26},{... | collective-permute-start | bytes 1179656 | tf_op jit(solution)/shard_map/while/body/eval_jaxpr/ppermute | solution.py:35
  201.0 6.3 %collective-permute-done = bf16[32,6144]{1,0:T(8,128)(2,1)S(1)} collective-permute-done((bf16[32,6144]{1,0:T(8,128)(2,1)}, bf16[32,6144]{1,0:T(8,128)(2,1)S(1)}, u32[]{:S(2)}, u32[]{:S(2)}) %collective-permute-start) | collective-permute-done | bytes 393248 | tf_op jit(solution)/shard_map/while/body/eval_jaxpr/ppermute | solution.py:35
  208.7 4.5 collective-permute-start
  213.3 5.6 %collective-permute-done = bf16[32,6144]{1,0:T(8,128)(2,1)S(1)} collective-permute-done((bf16[32,6144]{1,0:T(8,128)(2,1)}, bf16[32,6144]{1,0:T(8,128)(2,1)S(1)}, u32[]{:S(2)}, u32[]{:S(2)}) %collective-permute-start) | collective-permute-done | bytes 393248 | tf_op jit(solution)/shard_map/while/body/eval_jaxpr/ppermute | solution.py:35
  220.3 13.7 %collective-permute-start = (bf16[32,6144]{1,0:T(8,128)(2,1)}, bf16[32,6144]{1,0:T(8,128)(2,1)S(1)}, u32[]{:S(2)}, u32[]{:S(2)}) collective-permute-start(bf16[32,6144]{1,0:T(8,128)(2,1)} %get-tuple-element.1007), channel_id=1, source_target_pairs={{0,8},{8,16},{16,24},{1,9},{9,17},{17,25},{2,10},{10,18},{18,26},{... | collective-permute-start | bytes 1179656 | tf_op jit(solution)/shard_map/while/body/eval_jaxpr/ppermute | solution.py:35
  234.1 5.6 %collective-permute-done = bf16[32,6144]{1,0:T(8,128)(2,1)S(1)} collective-permute-done((bf16[32,6144]{1,0:T(8,128)(2,1)}, bf16[32,6144]{1,0:T(8,128)(2,1)S(1)}, u32[]{:S(2)}, u32[]{:S(2)}) %collective-permute-start) | collective-permute-done | bytes 393248 | tf_op jit(solution)/shard_map/while/body/eval_jaxpr/ppermute | solution.py:35
  247.9 201.3 %while.47 = (s32[]{:T(128)}, bf16[32,6144]{1,0:T(8,128)(2,1)S(1)}, bf16[6,32,6144]{2,1,0:T(8,128)(2,1)}, bf16[6,32,256]{2,1,0:T(8,128)(2,1)}, bf16[6,32,6144]{2,...) while((s32[]{:T(128)}, bf16[32,6144]{1,0:T(8,128)(2,1)S(1)}, ...), condition=%wide.region_11.12_spmd, body=%wide.region_5.11_spmd.sunk | while | flops 307413088 | bytes 30807244 | solution.py:156
  250.0 13.5 %collective-permute-done.1 = bf16[32,6144]{1,0:T(8,128)(2,1)S(1)} collective-permute-done((bf16[32,6144]{1,0:T(8,128)(2,1)}, bf16[32,6144]{1,0:T(8,128)(2,1)S(1)}, u32[]{:S(2)}, u32[]{:S(2)}) %collective-permute-start.1) | collective-permute-done | bytes 393248 | tf_op jit(solution)/shard_map/while/body/eval_jaxpr/ppermute | solution.py:35
  265.5 8.6 %collective-permute-done.1 = bf16[32,6144]{1,0:T(8,128)(2,1)S(1)} collective-permute-done((bf16[32,6144]{1,0:T(8,128)(2,1)}, bf16[32,6144]{1,0:T(8,128)(2,1)S(1)}, u32[]{:S(2)}, u32[]{:S(2)}) %collective-permute-start.1) | collective-permute-done | bytes 393248 | tf_op jit(solution)/shard_map/while/body/eval_jaxpr/ppermute | solution.py:35
  276.2 37.8 %collective-permute-done.1 = bf16[32,6144]{1,0:T(8,128)(2,1)S(1)} collective-permute-done((bf16[32,6144]{1,0:T(8,128)(2,1)}, bf16[32,6144]{1,0:T(8,128)(2,1)S(1)}, u32[]{:S(2)}, u32[]{:S(2)}) %collective-permute-start.1) | collective-permute-done | bytes 393248 | tf_op jit(solution)/shard_map/while/body/eval_jaxpr/ppermute | solution.py:35
  314.0 11.4 %conditional.5 = (bf16[32,6144]{1,0:T(8,128)(2,1)}, bf16[6,32,6144]{2,1,0:T(8,128)(2,1)}, bf16[6,32,256]{2,1,0:T(8,128)(2,1)}, bf16[6,32,6144]{2,1,0:T(8,128)(2,...) conditional(s32[]{:T(128)} %convert_element_type.184, ...), branch_computations={%region_6.6_spmd, %region_7.10_spmd} | conditional | flops 307413088 | bytes 29233976 | solution.py:150
  326.7 9.4 %collective-permute-done.1 = bf16[32,6144]{1,0:T(8,128)(2,1)S(1)} collective-permute-done((bf16[32,6144]{1,0:T(8,128)(2,1)}, bf16[32,6144]{1,0:T(8,128)(2,1)S(1)}, u32[]{:S(2)}, u32[]{:S(2)}) %collective-permute-start.1) | collective-permute-done | bytes 393248 | tf_op jit(solution)/shard_map/while/body/eval_jaxpr/ppermute | solution.py:35
  336.1 11.3 %conditional.5 = (bf16[32,6144]{1,0:T(8,128)(2,1)}, bf16[6,32,6144]{2,1,0:T(8,128)(2,1)}, bf16[6,32,256]{2,1,0:T(8,128)(2,1)}, bf16[6,32,6144]{2,1,0:T(8,128)(2,...) conditional(s32[]{:T(128)} %convert_element_type.184, ...), branch_computations={%region_6.6_spmd, %region_7.10_spmd} | conditional | flops 307413088 | bytes 29233976 | solution.py:150
  348.7 9.5 %collective-permute-done.1 = bf16[32,6144]{1,0:T(8,128)(2,1)S(1)} collective-permute-done((bf16[32,6144]{1,0:T(8,128)(2,1)}, bf16[32,6144]{1,0:T(8,128)(2,1)S(1)}, u32[]{:S(2)}, u32[]{:S(2)}) %collective-permute-start.1) | collective-permute-done | bytes 393248 | tf_op jit(solution)/shard_map/while/body/eval_jaxpr/ppermute | solution.py:35
  358.2 11.4 %conditional.5 = (bf16[32,6144]{1,0:T(8,128)(2,1)}, bf16[6,32,6144]{2,1,0:T(8,128)(2,1)}, bf16[6,32,256]{2,1,0:T(8,128)(2,1)}, bf16[6,32,6144]{2,1,0:T(8,128)(2,...) conditional(s32[]{:T(128)} %convert_element_type.184, ...), branch_computations={%region_6.6_spmd, %region_7.10_spmd} | conditional | flops 307413088 | bytes 29233976 | solution.py:150
  370.9 9.5 %collective-permute-done.1 = bf16[32,6144]{1,0:T(8,128)(2,1)S(1)} collective-permute-done((bf16[32,6144]{1,0:T(8,128)(2,1)}, bf16[32,6144]{1,0:T(8,128)(2,1)S(1)}, u32[]{:S(2)}, u32[]{:S(2)}) %collective-permute-start.1) | collective-permute-done | bytes 393248 | tf_op jit(solution)/shard_map/while/body/eval_jaxpr/ppermute | solution.py:35
  380.3 11.4 %conditional.5 = (bf16[32,6144]{1,0:T(8,128)(2,1)}, bf16[6,32,6144]{2,1,0:T(8,128)(2,1)}, bf16[6,32,256]{2,1,0:T(8,128)(2,1)}, bf16[6,32,6144]{2,1,0:T(8,128)(2,...) conditional(s32[]{:T(128)} %convert_element_type.184, ...), branch_computations={%region_6.6_spmd, %region_7.10_spmd} | conditional | flops 307413088 | bytes 29233976 | solution.py:150
  393.0 9.9 %collective-permute-done.1 = bf16[32,6144]{1,0:T(8,128)(2,1)S(1)} collective-permute-done((bf16[32,6144]{1,0:T(8,128)(2,1)}, bf16[32,6144]{1,0:T(8,128)(2,1)S(1)}, u32[]{:S(2)}, u32[]{:S(2)}) %collective-permute-start.1) | collective-permute-done | bytes 393248 | tf_op jit(solution)/shard_map/while/body/eval_jaxpr/ppermute | solution.py:35
  402.9 11.4 %conditional.5 = (bf16[32,6144]{1,0:T(8,128)(2,1)}, bf16[6,32,6144]{2,1,0:T(8,128)(2,1)}, bf16[6,32,256]{2,1,0:T(8,128)(2,1)}, bf16[6,32,6144]{2,1,0:T(8,128)(2,...) conditional(s32[]{:T(128)} %convert_element_type.184, ...), branch_computations={%region_6.6_spmd, %region_7.10_spmd} | conditional | flops 307413088 | bytes 29233976 | solution.py:150
  415.5 12.4 %collective-permute-done.1 = bf16[32,6144]{1,0:T(8,128)(2,1)S(1)} collective-permute-done((bf16[32,6144]{1,0:T(8,128)(2,1)}, bf16[32,6144]{1,0:T(8,128)(2,1)S(1)}, u32[]{:S(2)}, u32[]{:S(2)}) %collective-permute-start.1) | collective-permute-done | bytes 393248 | tf_op jit(solution)/shard_map/while/body/eval_jaxpr/ppermute | solution.py:35
  428.0 11.4 %conditional.5 = (bf16[32,6144]{1,0:T(8,128)(2,1)}, bf16[6,32,6144]{2,1,0:T(8,128)(2,1)}, bf16[6,32,256]{2,1,0:T(8,128)(2,1)}, bf16[6,32,6144]{2,1,0:T(8,128)(2,...) conditional(s32[]{:T(128)} %convert_element_type.184, ...), branch_computations={%region_6.6_spmd, %region_7.10_spmd} | conditional | flops 307413088 | bytes 29233976 | solution.py:150
  440.6 8.6 %collective-permute-done.1 = bf16[32,6144]{1,0:T(8,128)(2,1)S(1)} collective-permute-done((bf16[32,6144]{1,0:T(8,128)(2,1)}, bf16[32,6144]{1,0:T(8,128)(2,1)S(1)}, u32[]{:S(2)}, u32[]{:S(2)}) %collective-permute-start.1) | collective-permute-done | bytes 393248 | tf_op jit(solution)/shard_map/while/body/eval_jaxpr/ppermute | solution.py:35
  457.8 41.5 %psum.7 = f32[1,6144]{1,0:T(1,128)} all-reduce(f32[1,6144]{1,0:T(1,128)S(1)} %bitcast.98), channel_id=1, replica_groups=mesh['section'=4,'rep'=8] {'rep'}, use_global_device_ids=true, to_apply=%region_13.14 | all-reduce | flops 6144 | bytes 49152 | tf_op jit(solution)/shard_map/psum | solution.py:180
  499.3 41.1 %reduce-scatter.2.cloned.1.call-done = bf16[768,512]{0,1:T(8,128)(2,1)} async-done(((bf16[6144,512]{0,1:T(8,128)(2,1)}), bf16[768,512]{0,1:T(8,128)(2,1)}) %reduce-scatter.2.cloned.1.call-update) | async-done | bytes 786448 | tf_op jit(solution)/shard_map/reduce_scatter | solution.py:172
  (208 shorter events, 175.5 us)
Async XLA Ops:
  7.2 71.2 %all-gather.3.cloned.1.call-start = ((), (), s32[]{:S(2)}) async-start(), calls=%async_computation.2 | async-start | bytes 3538944 | tf_op jit(solution)/shard_map/all_gather | solution.py:89
  7.9 532.6 %reduce-scatter.2.cloned.1.call-start = ((), (), s32[]{:S(2)}) async-start(), calls=%async_computation.1 | async-start | bytes 7077888 | tf_op jit(solution)/shard_map/reduce_scatter | solution.py:172
  7.9 10.2 %collective-permute-start.2 = (bf16[768,256]{1,0:T(8,128)(2,1)}, bf16[768,256]{1,0:T(8,128)(2,1)S(1)}, u32[]{:S(2)}, u32[]{:S(2)}) collective-permute-start(bf16[768,256]{1,0:T(8,128)(2,1)} %bitcast.96), channel_id=1, source_target_pairs={{0,1},{1,2},{2,3},{3,4},{4,5},{5,6},{6,7},{7,0},{8,9},{9,10},{10,1... | collective-permute-start | bytes 1179656 | tf_op jit(solution)/shard_map/ppermute | solution.py:23
  18.2 18.2 %collective-permute-start.3 = (bf16[768,256]{1,0:T(8,128)(2,1)S(1)}, bf16[768,256]{1,0:T(8,128)(2,1)S(1)}, u32[]{:S(2)}, u32[]{:S(2)}) collective-permute-start(bf16[768,256]{1,0:T(8,128)(2,1)S(1)} %collective-permute-done.2), channel_id=1, source_target_pairs={{0,1},{1,2},{2,3},{3,4},{4,5},{5,6},{6,7},{7,0},{8,9},{9,10},{10,1... | collective-permute-start | bytes 1179656 | tf_op jit(solution)/shard_map/ppermute | solution.py:23
  18.2 20.8 %collective-permute-start.6 = (bf16[768,256]{1,0:T(8,128)(2,1)}, bf16[768,256]{1,0:T(8,128)(2,1)S(1)}, u32[]{:S(2)}, u32[]{:S(2)}) collective-permute-start(bf16[768,256]{1,0:T(8,128)(2,1)} %bitcast.97), channel_id=1, source_target_pairs={{1,0},{2,1},{3,2},{4,3},{5,4},{6,5},{7,6},{0,7},{9,8},{10,9},{11,1... | collective-permute-start | bytes 1179656 | tf_op jit(solution)/shard_map/ppermute | solution.py:25
  36.4 19.6 %collective-permute-start.4 = (bf16[768,256]{1,0:T(8,128)(2,1)S(1)}, bf16[768,256]{1,0:T(8,128)(2,1)S(1)}, u32[]{:S(2)}, u32[]{:S(2)}) collective-permute-start(bf16[768,256]{1,0:T(8,128)(2,1)S(1)} %collective-permute-done.3), channel_id=1, source_target_pairs={{0,1},{1,2},{2,3},{3,4},{4,5},{5,6},{6,7},{7,0},{8,9},{9,10},{10,1... | collective-permute-start | bytes 1179656 | tf_op jit(solution)/shard_map/ppermute | solution.py:23
  37.1 35.4 %copy-start.9 = (bf16[1,768,256]{2,1,0:T(8,128)(2,1)S(1)}, bf16[1,768,256]{2,1,0:T(8,128)(2,1)}, u32[]{:S(2)}) copy-start(bf16[1,768,256]{2,1,0:T(8,128)(2,1)} %param.17) | copy-start | bytes 1179652
  39.0 20.6 %collective-permute-start.7 = (bf16[768,256]{1,0:T(8,128)(2,1)S(1)}, bf16[768,256]{1,0:T(8,128)(2,1)S(1)}, u32[]{:S(2)}, u32[]{:S(2)}) collective-permute-start(bf16[768,256]{1,0:T(8,128)(2,1)S(1)} %collective-permute-done.6), channel_id=1, source_target_pairs={{1,0},{2,1},{3,2},{4,3},{5,4},{6,5},{7,6},{0,7},{9,8},{10,9},{11,1... | collective-permute-start | bytes 1179656 | tf_op jit(solution)/shard_map/ppermute | solution.py:25
  56.0 13.5 %collective-permute-start.5 = (bf16[768,256]{1,0:T(8,128)(2,1)S(1)}, bf16[768,256]{1,0:T(8,128)(2,1)S(1)}, u32[]{:S(2)}, u32[]{:S(2)}) collective-permute-start(bf16[768,256]{1,0:T(8,128)(2,1)S(1)} %collective-permute-done.4), channel_id=1, source_target_pairs={{0,1},{1,2},{2,3},{3,4},{4,5},{5,6},{6,7},{7,0},{8,9},{9,10},{10,1... | collective-permute-start | bytes 1179656 | tf_op jit(solution)/shard_map/ppermute | solution.py:23
  59.6 15.3 %collective-permute-start.8 = (bf16[768,256]{1,0:T(8,128)(2,1)S(1)}, bf16[768,256]{1,0:T(8,128)(2,1)S(1)}, u32[]{:S(2)}, u32[]{:S(2)}) collective-permute-start(bf16[768,256]{1,0:T(8,128)(2,1)S(1)} %collective-permute-done.7), channel_id=1, source_target_pairs={{1,0},{2,1},{3,2},{4,3},{5,4},{6,5},{7,6},{0,7},{9,8},{10,9},{11,1... | collective-permute-start | bytes 1179656 | tf_op jit(solution)/shard_map/ppermute | solution.py:25
  87.8 8.9 %collective-permute-start = (bf16[32,6144]{1,0:T(8,128)(2,1)}, bf16[32,6144]{1,0:T(8,128)(2,1)S(1)}, u32[]{:S(2)}, u32[]{:S(2)}) collective-permute-start(bf16[32,6144]{1,0:T(8,128)(2,1)} %get-tuple-element.1007), channel_id=1, source_target_pairs={{0,8},{8,16},{16,24},{1,9},{9,17},{17,25},{2,10},{10,18},{18,26},{... | collective-permute-start | bytes 1179656 | tf_op jit(solution)/shard_map/while/body/eval_jaxpr/ppermute | solution.py:35
  104.5 11.2 %collective-permute-start = (bf16[32,6144]{1,0:T(8,128)(2,1)}, bf16[32,6144]{1,0:T(8,128)(2,1)S(1)}, u32[]{:S(2)}, u32[]{:S(2)}) collective-permute-start(bf16[32,6144]{1,0:T(8,128)(2,1)} %get-tuple-element.1007), channel_id=1, source_target_pairs={{0,8},{8,16},{16,24},{1,9},{9,17},{17,25},{2,10},{10,18},{18,26},{... | collective-permute-start | bytes 1179656 | tf_op jit(solution)/shard_map/while/body/eval_jaxpr/ppermute | solution.py:35
  123.4 10.3 %collective-permute-start = (bf16[32,6144]{1,0:T(8,128)(2,1)}, bf16[32,6144]{1,0:T(8,128)(2,1)S(1)}, u32[]{:S(2)}, u32[]{:S(2)}) collective-permute-start(bf16[32,6144]{1,0:T(8,128)(2,1)} %get-tuple-element.1007), channel_id=1, source_target_pairs={{0,8},{8,16},{16,24},{1,9},{9,17},{17,25},{2,10},{10,18},{18,26},{... | collective-permute-start | bytes 1179656 | tf_op jit(solution)/shard_map/while/body/eval_jaxpr/ppermute | solution.py:35
  141.5 10.0 %collective-permute-start = (bf16[32,6144]{1,0:T(8,128)(2,1)}, bf16[32,6144]{1,0:T(8,128)(2,1)S(1)}, u32[]{:S(2)}, u32[]{:S(2)}) collective-permute-start(bf16[32,6144]{1,0:T(8,128)(2,1)} %get-tuple-element.1007), channel_id=1, source_target_pairs={{0,8},{8,16},{16,24},{1,9},{9,17},{17,25},{2,10},{10,18},{18,26},{... | collective-permute-start | bytes 1179656 | tf_op jit(solution)/shard_map/while/body/eval_jaxpr/ppermute | solution.py:35
  159.2 10.0 %collective-permute-start = (bf16[32,6144]{1,0:T(8,128)(2,1)}, bf16[32,6144]{1,0:T(8,128)(2,1)S(1)}, u32[]{:S(2)}, u32[]{:S(2)}) collective-permute-start(bf16[32,6144]{1,0:T(8,128)(2,1)} %get-tuple-element.1007), channel_id=1, source_target_pairs={{0,8},{8,16},{16,24},{1,9},{9,17},{17,25},{2,10},{10,18},{18,26},{... | collective-permute-start | bytes 1179656 | tf_op jit(solution)/shard_map/while/body/eval_jaxpr/ppermute | solution.py:35
  177.0 10.9 %collective-permute-start = (bf16[32,6144]{1,0:T(8,128)(2,1)}, bf16[32,6144]{1,0:T(8,128)(2,1)S(1)}, u32[]{:S(2)}, u32[]{:S(2)}) collective-permute-start(bf16[32,6144]{1,0:T(8,128)(2,1)} %get-tuple-element.1007), channel_id=1, source_target_pairs={{0,8},{8,16},{16,24},{1,9},{9,17},{17,25},{2,10},{10,18},{18,26},{... | collective-permute-start | bytes 1179656 | tf_op jit(solution)/shard_map/while/body/eval_jaxpr/ppermute | solution.py:35
  189.4 17.8 %collective-permute-start = (bf16[32,6144]{1,0:T(8,128)(2,1)}, bf16[32,6144]{1,0:T(8,128)(2,1)S(1)}, u32[]{:S(2)}, u32[]{:S(2)}) collective-permute-start(bf16[32,6144]{1,0:T(8,128)(2,1)} %get-tuple-element.1007), channel_id=1, source_target_pairs={{0,8},{8,16},{16,24},{1,9},{9,17},{17,25},{2,10},{10,18},{18,26},{... | collective-permute-start | bytes 1179656 | tf_op jit(solution)/shard_map/while/body/eval_jaxpr/ppermute | solution.py:35
  208.7 10.1 %collective-permute-start = (bf16[32,6144]{1,0:T(8,128)(2,1)}, bf16[32,6144]{1,0:T(8,128)(2,1)S(1)}, u32[]{:S(2)}, u32[]{:S(2)}) collective-permute-start(bf16[32,6144]{1,0:T(8,128)(2,1)} %get-tuple-element.1007), channel_id=1, source_target_pairs={{0,8},{8,16},{16,24},{1,9},{9,17},{17,25},{2,10},{10,18},{18,26},{... | collective-permute-start | bytes 1179656 | tf_op jit(solution)/shard_map/while/body/eval_jaxpr/ppermute | solution.py:35
  220.3 19.3 %collective-permute-start = (bf16[32,6144]{1,0:T(8,128)(2,1)}, bf16[32,6144]{1,0:T(8,128)(2,1)S(1)}, u32[]{:S(2)}, u32[]{:S(2)}) collective-permute-start(bf16[32,6144]{1,0:T(8,128)(2,1)} %get-tuple-element.1007), channel_id=1, source_target_pairs={{0,8},{8,16},{16,24},{1,9},{9,17},{17,25},{2,10},{10,18},{18,26},{... | collective-permute-start | bytes 1179656 | tf_op jit(solution)/shard_map/while/body/eval_jaxpr/ppermute | solution.py:35
  242.8 5.2 copy-start
  248.7 14.8 %collective-permute-start.1 = (bf16[32,6144]{1,0:T(8,128)(2,1)}, bf16[32,6144]{1,0:T(8,128)(2,1)S(1)}, u32[]{:S(2)}, u32[]{:S(2)}) collective-permute-start(bf16[32,6144]{1,0:T(8,128)(2,1)} %get-tuple-element.1024), channel_id=1, source_target_pairs={{8,0},{16,8},{24,16},{9,1},{17,9},{25,17},{10,2},{18,10},{26,18},{... | collective-permute-start | bytes 1179656 | tf_op jit(solution)/shard_map/while/body/eval_jaxpr/ppermute | solution.py:35
  264.2 9.9 %collective-permute-start.1 = (bf16[32,6144]{1,0:T(8,128)(2,1)}, bf16[32,6144]{1,0:T(8,128)(2,1)S(1)}, u32[]{:S(2)}, u32[]{:S(2)}) collective-permute-start(bf16[32,6144]{1,0:T(8,128)(2,1)} %get-tuple-element.1024), channel_id=1, source_target_pairs={{8,0},{16,8},{24,16},{9,1},{17,9},{25,17},{10,2},{18,10},{26,18},{... | collective-permute-start | bytes 1179656 | tf_op jit(solution)/shard_map/while/body/eval_jaxpr/ppermute | solution.py:35
  274.9 39.1 %collective-permute-start.1 = (bf16[32,6144]{1,0:T(8,128)(2,1)}, bf16[32,6144]{1,0:T(8,128)(2,1)S(1)}, u32[]{:S(2)}, u32[]{:S(2)}) collective-permute-start(bf16[32,6144]{1,0:T(8,128)(2,1)} %get-tuple-element.1024), channel_id=1, source_target_pairs={{8,0},{16,8},{24,16},{9,1},{17,9},{25,17},{10,2},{18,10},{26,18},{... | collective-permute-start | bytes 1179656 | tf_op jit(solution)/shard_map/while/body/eval_jaxpr/ppermute | solution.py:35
  314.0 5.6 %copy-start.2 = (bf16[6144,256]{1,0:T(8,128)(2,1)S(1)}, bf16[6144,256]{1,0:T(8,128)(2,1)}, u32[]{:S(2)}) copy-start(bf16[6144,256]{1,0:T(8,128)(2,1)} %get-tuple-element.747) | copy-start | bytes 9437188 | tf_op jit(solution)/shard_map/while/body/eval_jaxpr/cond
  319.6 3.4 copy-start.5
  323.0 2.4 copy-start.6
  325.4 10.7 %collective-permute-start.1 = (bf16[32,6144]{1,0:T(8,128)(2,1)}, bf16[32,6144]{1,0:T(8,128)(2,1)S(1)}, u32[]{:S(2)}, u32[]{:S(2)}) collective-permute-start(bf16[32,6144]{1,0:T(8,128)(2,1)} %get-tuple-element.1024), channel_id=1, source_target_pairs={{8,0},{16,8},{24,16},{9,1},{17,9},{25,17},{10,2},{18,10},{26,18},{... | collective-permute-start | bytes 1179656 | tf_op jit(solution)/shard_map/while/body/eval_jaxpr/ppermute | solution.py:35
  336.1 5.5 %copy-start.2 = (bf16[6144,256]{1,0:T(8,128)(2,1)S(1)}, bf16[6144,256]{1,0:T(8,128)(2,1)}, u32[]{:S(2)}) copy-start(bf16[6144,256]{1,0:T(8,128)(2,1)} %get-tuple-element.747) | copy-start | bytes 9437188 | tf_op jit(solution)/shard_map/while/body/eval_jaxpr/cond
  341.6 3.4 copy-start.5
  347.4 10.8 %collective-permute-start.1 = (bf16[32,6144]{1,0:T(8,128)(2,1)}, bf16[32,6144]{1,0:T(8,128)(2,1)S(1)}, u32[]{:S(2)}, u32[]{:S(2)}) collective-permute-start(bf16[32,6144]{1,0:T(8,128)(2,1)} %get-tuple-element.1024), channel_id=1, source_target_pairs={{8,0},{16,8},{24,16},{9,1},{17,9},{25,17},{10,2},{18,10},{26,18},{... | collective-permute-start | bytes 1179656 | tf_op jit(solution)/shard_map/while/body/eval_jaxpr/ppermute | solution.py:35
  358.2 5.5 %copy-start.2 = (bf16[6144,256]{1,0:T(8,128)(2,1)S(1)}, bf16[6144,256]{1,0:T(8,128)(2,1)}, u32[]{:S(2)}) copy-start(bf16[6144,256]{1,0:T(8,128)(2,1)} %get-tuple-element.747) | copy-start | bytes 9437188 | tf_op jit(solution)/shard_map/while/body/eval_jaxpr/cond
  363.7 3.4 copy-start.5
  367.2 2.4 copy-start.6
  369.6 10.8 %collective-permute-start.1 = (bf16[32,6144]{1,0:T(8,128)(2,1)}, bf16[32,6144]{1,0:T(8,128)(2,1)S(1)}, u32[]{:S(2)}, u32[]{:S(2)}) collective-permute-start(bf16[32,6144]{1,0:T(8,128)(2,1)} %get-tuple-element.1024), channel_id=1, source_target_pairs={{8,0},{16,8},{24,16},{9,1},{17,9},{25,17},{10,2},{18,10},{26,18},{... | collective-permute-start | bytes 1179656 | tf_op jit(solution)/shard_map/while/body/eval_jaxpr/ppermute | solution.py:35
  380.3 5.5 %copy-start.2 = (bf16[6144,256]{1,0:T(8,128)(2,1)S(1)}, bf16[6144,256]{1,0:T(8,128)(2,1)}, u32[]{:S(2)}) copy-start(bf16[6144,256]{1,0:T(8,128)(2,1)} %get-tuple-element.747) | copy-start | bytes 9437188 | tf_op jit(solution)/shard_map/while/body/eval_jaxpr/cond
  385.8 3.4 copy-start.5
  389.3 2.4 copy-start.6
  391.7 11.2 %collective-permute-start.1 = (bf16[32,6144]{1,0:T(8,128)(2,1)}, bf16[32,6144]{1,0:T(8,128)(2,1)S(1)}, u32[]{:S(2)}, u32[]{:S(2)}) collective-permute-start(bf16[32,6144]{1,0:T(8,128)(2,1)} %get-tuple-element.1024), channel_id=1, source_target_pairs={{8,0},{16,8},{24,16},{9,1},{17,9},{25,17},{10,2},{18,10},{26,18},{... | collective-permute-start | bytes 1179656 | tf_op jit(solution)/shard_map/while/body/eval_jaxpr/ppermute | solution.py:35
  402.9 5.5 %copy-start.2 = (bf16[6144,256]{1,0:T(8,128)(2,1)S(1)}, bf16[6144,256]{1,0:T(8,128)(2,1)}, u32[]{:S(2)}) copy-start(bf16[6144,256]{1,0:T(8,128)(2,1)} %get-tuple-element.747) | copy-start | bytes 9437188 | tf_op jit(solution)/shard_map/while/body/eval_jaxpr/cond
  408.4 3.4 copy-start.5
  411.9 2.4 copy-start.6
  414.3 13.7 %collective-permute-start.1 = (bf16[32,6144]{1,0:T(8,128)(2,1)}, bf16[32,6144]{1,0:T(8,128)(2,1)S(1)}, u32[]{:S(2)}, u32[]{:S(2)}) collective-permute-start(bf16[32,6144]{1,0:T(8,128)(2,1)} %get-tuple-element.1024), channel_id=1, source_target_pairs={{8,0},{16,8},{24,16},{9,1},{17,9},{25,17},{10,2},{18,10},{26,18},{... | collective-permute-start | bytes 1179656 | tf_op jit(solution)/shard_map/while/body/eval_jaxpr/ppermute | solution.py:35
  428.0 5.5 %copy-start.2 = (bf16[6144,256]{1,0:T(8,128)(2,1)S(1)}, bf16[6144,256]{1,0:T(8,128)(2,1)}, u32[]{:S(2)}) copy-start(bf16[6144,256]{1,0:T(8,128)(2,1)} %get-tuple-element.747) | copy-start | bytes 9437188 | tf_op jit(solution)/shard_map/while/body/eval_jaxpr/cond
  433.5 3.4 copy-start.5
  437.0 2.4 copy-start.6
  439.3 9.9 %collective-permute-start.1 = (bf16[32,6144]{1,0:T(8,128)(2,1)}, bf16[32,6144]{1,0:T(8,128)(2,1)S(1)}, u32[]{:S(2)}, u32[]{:S(2)}) collective-permute-start(bf16[32,6144]{1,0:T(8,128)(2,1)} %get-tuple-element.1024), channel_id=1, source_target_pairs={{8,0},{16,8},{24,16},{9,1},{17,9},{25,17},{10,2},{18,10},{26,18},{... | collective-permute-start | bytes 1179656 | tf_op jit(solution)/shard_map/while/body/eval_jaxpr/ppermute | solution.py:35
  449.2 2.9 copy-start.4
  449.2 2.9 copy-start.8
  (12 other events, 12.2 us)
Sparse Core Ops, SparseCore 0:
  9.6 55.5 all-gather.2
  457.2 83.2 reduce-scatter.1
